TPU v7x, 128 devices: a whole 4x4x4 slice. The times are simulated.
128 devices in a mesh: seq: 16 (over z, y), head: 8 (over x, core).
Axes of the slice: x: 4, y: 4, z: 4, core: 2. Of those that a mesh axis runs over, the one named last changes fastest.
Arguments:
- normed: bfloat16 [32, 8192], P(None, 'seq'), may hold values from -6 to 6
- qkv_weight: bfloat16 [8192, 10240], P('seq', 'head'), may hold values from -0.0625 to 0.0625
- out_weight: bfloat16 [8192, 8192], P('head', 'seq'), may hold values from -0.0625 to 0.0625
- kv_cache: bfloat16 [1024, 2, 128, 1024], P('seq', None, None, 'head'), may hold values from -160 to 160
- lengths: int32 [8], replicated, may hold values from 1 to 9344, as said below
- slot_request: int32 [1024], P('seq'), may hold values from 0 to 8, as said below
- slot_block: int32 [1024], P('seq'), may hold values from 0 to 72, as said below
- send_list: int32 [16, 16, 4], P('seq'), may hold values from 0 to 64, as said below
- recv_list: int32 [16, 16, 4], P('seq'), may hold values from 0 to 64, as said below
Outputs:
- projected: bfloat16 [32, 8192], P('head', 'seq')
- moved_cache: bfloat16 [1024, 2, 128, 1024], P('seq', None, None, 'head')
Inputs may be any that keep to these rules, and one draw needn't show every extreme that they name: `lengths`: every request has at least one block; a request with n blocks has each of the block numbers 0 to n - 1 in exactly one slot, and its length lies in ((n - 1) * 128, n * 128]. `slot_request`: 8 marks an empty slot. `slot_block`: 0 in empty slots. 64 marks an unused entry, and send_list[s, e, c] is unused exactly where recv_list[e, s, c] is; every owned slot is sent exactly once and no empty slot is sent; at most 4 blocks go from one device to another, and some device receives exactly 4 from every device; after the scale-in only half of the seq devices hold blocks. `recv_list`: 64 marks an unused entry; each slot of a device is filled at most once.
All inputs are finite; a program needn't handle non-finite values.
Results may differ from a plain program's by a relative error of at most 0.025.
Values may be sent and summed in bfloat16 or wider, within the bound.
A program may use at most 128 MiB of HBM per device.

v0:
```python
import jax
import jax.numpy as jnp
from jax import lax
from jax.sharding import PartitionSpec as P

HEADS = 64
KV_HEADS = 8
HEAD = 128
POS = 4
BLOCK = 128
rope_base = 500000.0
neg_large = -1e30


def rotate(values, positions):
    half_width = values.shape[-1] // 2
    frequencies = rope_base ** (
        -(jnp.arange(half_width, dtype=jnp.float32) * 2.0 / values.shape[-1])
    )
    angles = positions[..., None] * frequencies
    cosine_table = jnp.cos(angles)
    sine_table = jnp.sin(angles)
    lower_half = values[..., :half_width]
    upper_half = values[..., half_width:]
    return jnp.concatenate(
        [
            lower_half * cosine_table - upper_half * sine_table,
            upper_half * cosine_table + lower_half * sine_table,
        ],
        axis=-1,
    )


def body(
    normed,
    qkv_weight,
    out_weight,
    kv_cache,
    lengths,
    slot_request,
    slot_block,
    send_list,
    recv_list,
):
    group_size = HEADS // KV_HEADS
    scale_factor = HEAD ** (-0.5)
    requests = lengths.shape[0]
    slot_count = kv_cache.shape[0]
    full_rows = lax.all_gather(normed, "seq", axis=1, tiled=True)
    projected_qkv = jnp.dot(
        full_rows,
        lax.all_gather(qkv_weight, "seq", axis=0, tiled=True),
        preferred_element_type=jnp.float32,
    )
    projected_qkv = projected_qkv.reshape(requests, POS, -1, group_size + 2, HEAD)
    local_kv = projected_qkv.shape[2]
    positions = (lengths[:, None] + jnp.arange(POS, dtype=jnp.int32)[None, :]).astype(jnp.float32)
    queries = rotate(projected_qkv[:, :, :, :group_size], positions[:, :, None, None]).astype(
        jnp.bfloat16
    )
    keys_new = rotate(projected_qkv[:, :, :, group_size], positions[:, :, None]).astype(
        jnp.bfloat16
    )
    values_new = projected_qkv[:, :, :, group_size + 1].astype(jnp.bfloat16)
    flat_send = send_list.reshape(-1)
    outgoing = kv_cache[jnp.minimum(flat_send, slot_count - 1)]
    outgoing = outgoing.reshape((lax.axis_size("seq"), -1) + kv_cache.shape[1:])
    incoming = lax.all_to_all(outgoing, "seq", split_axis=0, concat_axis=0, tiled=True)
    incoming = incoming.reshape((-1,) + kv_cache.shape[1:])
    moved_cache = jnp.zeros_like(kv_cache).at[recv_list.reshape(-1)].set(incoming, mode="drop")
    slot_clip = jnp.minimum(slot_request, requests - 1)
    live_slot = slot_request < requests
    token_pos = slot_block[:, None] * BLOCK + jnp.arange(BLOCK, dtype=jnp.int32)[None, :]
    token_valid = (token_pos < lengths[slot_clip][:, None]) & live_slot[:, None]
    cache_view = kv_cache.reshape(slot_count, 2, BLOCK, local_kv, HEAD)
    gathered = queries[slot_clip]
    scores = (
        jnp.einsum(
            "sptgd,sbtd->stgpb", gathered, cache_view[:, 0], preferred_element_type=jnp.float32
        )
        * scale_factor
    )
    scores = jnp.where(token_valid[:, None, None, None, :], scores, neg_large)
    slot_max = jnp.max(scores, axis=-1)
    weights = jnp.where(
        token_valid[:, None, None, None, :], jnp.exp(scores - slot_max[..., None]), 0.0
    )
    slot_sum = jnp.sum(weights, axis=-1)
    slot_acc = jnp.einsum(
        "stgpb,sbtd->stgpd",
        weights.astype(jnp.bfloat16),
        cache_view[:, 1],
        preferred_element_type=jnp.float32,
    )
    flat_width = local_kv * group_size * POS
    slot_max_flat = slot_max.reshape(slot_count, flat_width)
    member = slot_request[:, None] == jnp.arange(requests, dtype=jnp.int32)[None, :]
    request_max = jnp.max(
        jnp.where(member[:, None, :], slot_max_flat[:, :, None], neg_large), axis=0
    ).T
    rescale = jnp.exp(slot_max_flat - request_max[slot_clip])
    member_float = member.astype(jnp.float32).T
    request_sum = jnp.dot(
        member_float,
        slot_sum.reshape(slot_count, flat_width) * rescale,
        precision=lax.Precision.HIGHEST,
    )
    scaled_acc = (slot_acc.reshape(slot_count, flat_width, HEAD) * rescale[:, :, None]).reshape(
        slot_count, flat_width * HEAD
    )
    request_acc = jnp.dot(member_float, scaled_acc, precision=lax.Precision.HIGHEST).reshape(
        requests, flat_width, HEAD
    )
    total_max = lax.pmax(request_max, "seq")
    adjust = jnp.exp(request_max - total_max)
    total_sum, total_acc = (
        lax.psum((request_sum * adjust).astype(jnp.bfloat16), "seq").astype(jnp.float32),
        lax.psum((request_acc * adjust[:, :, None]).astype(jnp.bfloat16), "seq").astype(
            jnp.float32
        ),
    )
    new_scores = (
        jnp.einsum("rptgd,rqtd->rtgpq", queries, keys_new, preferred_element_type=jnp.float32)
        * scale_factor
    )
    causal = jnp.arange(POS)[:, None] >= jnp.arange(POS)[None, :]
    new_scores = jnp.where(causal, new_scores, neg_large)
    cache_max = total_max.reshape(requests, local_kv, group_size, POS)
    top_max = jnp.maximum(cache_max, jnp.max(new_scores, axis=-1))
    carry_scale = jnp.exp(cache_max - top_max)
    new_weights = jnp.where(causal, jnp.exp(new_scores - top_max[..., None]), 0.0)
    denominator = total_sum.reshape(requests, local_kv, group_size, POS) * carry_scale + jnp.sum(
        new_weights, axis=-1
    )
    numerator = (
        total_acc.reshape(requests, local_kv, group_size, POS, HEAD) * carry_scale[..., None]
    )
    numerator = numerator + jnp.einsum(
        "rtgpq,rqtd->rtgpd",
        new_weights.astype(jnp.bfloat16),
        values_new,
        preferred_element_type=jnp.float32,
    )
    attended = (
        (numerator / denominator[..., None])
        .transpose(0, 3, 1, 2, 4)
        .reshape(requests * POS, -1)
        .astype(jnp.bfloat16)
    )
    projected = lax.psum_scatter(
        jnp.dot(attended, out_weight, preferred_element_type=jnp.float32).astype(jnp.bfloat16),
        "head",
        scatter_dimension=0,
        tiled=True,
    )
    return (projected, moved_cache)


def solution(mesh):
    placed = (
        P(None, "seq"),
        P("seq", "head"),
        P("head", "seq"),
        P("seq", None, None, "head"),
        P(),
        P("seq"),
        P("seq"),
        P("seq", None, None),
        P("seq", None, None),
    )
    return jax.shard_map(
        body,
        mesh=mesh,
        in_specs=placed,
        out_specs=(P("head", "seq"), P("seq", None, None, "head")),
        check_vma=False,
    )
```

profile of v0, /device:TPU:0, one launch (start us, length us, event | category | flops | bytes accessed | tf_op | source)
XLA Modules:
  0.0 363.6 jit_solution(1940336600849006869)
XLA Ops:
  7.2 0.0 copy-start
  7.2 0.0 all-gather.2.cloned.1.call-start
  7.2 0.7 all-gather.2.cloned.1.call-update
  7.9 0.7 broadcast_minimum_fusion
  8.6 0.1 copy.81
  8.7 0.1 min.26
  8.8 5.3 %gather_fusion.2 = bf16[64,2,128,128]{3,2,1,0:T(8,128)(2,1)} fusion(bf16[64,2,128,128]{3,2,1,0:T(8,128)(2,1)} %param.12, s32[1024]{0:T(1024)S(1)} %pad_clamp_fusion), kind=kCustom, calls=%fused_computation.2 | custom fusion | bytes 8388864 | tf_op jit(solution)/shard_map/gather | solution.py:66
  14.1 8.2 %all-to-all-start = ((bf16[16,4,2,128,128]{4,3,2,1,0:T(8,128)(2,1)}), bf16[16,4,2,128,128]{4,3,2,1,0:T(8,128)(2,1)}, u32[]{:S(2)}, u32[]{:S(2)}) async-start(bf16[16,4,2,128,128]{4,3,2,1,0:T(8,128)(2,1)} %bitcast.134), calls=%async_computation | async-start | bytes 8388608 | tf_op jit(solution)/shard_map/all_to_all | solution.py:68
  22.3 0.0 copy-start.9
  22.3 0.0 copy-start.12
  22.3 0.0 copy-start.3
  22.3 0.0 copy-start.7
  22.3 0.0 copy-start.11
  22.4 0.0 all-reduce.3.cloned.1.call-start
  22.4 5.2 %copy.111 = bf16[64,2,128,128]{3,2,0,1:T(8,128)(2,1)} copy(bf16[64,2,128,128]{3,2,1,0:T(8,128)(2,1)} %param.12) | data formatting | bytes 8388608 | tf_op args[3]
  27.6 0.1 copy.80
  27.7 0.1 reshape.425
  27.8 0.6 dynamic-slice
  29.1 0.6 iota_compare_fusion.3
  29.7 0.7 fusion.53
  30.3 4.8 %compare_select_fusion.3 = (s32[64]{0:T(128)S(1)}, s32[64]{0:T(128)S(1)}, s32[64]{0:T(128)S(1)}) fusion(s32[]{:T(128)} %bitcast.1, s32[]{:T(128)} %bitcast.2, s32[]{:T(128)} %bitcast.3, s32[]{:T(128)} %bitcast.4, s32[]{:T(128)} %bitcast.5, s32[]{:T(128)} %bitcast.6, s32[]{:T(128)} %bitcast.7, s32[]{:T(128)} %bitcast.8, s32[64]{0:T(128)S(1)} %copy-done.7, ...), kind=kLoop, calls=%fused_computation.87 | loop fusion | flops 1216 | bytes 1312 | tf_op jit(solution)/shard_map/gather | solution.py:74
  35.2 80.1 %all_gather.6 = bf16[32,8192]{1,0:T(8,128)(2,1)S(1)} all-gather(bf16[32,512]{1,0:T(8,128)(2,1)S(1)} %copy-done.6), channel_id=1, replica_groups=mesh['seq'=16,'head'=8] {'seq'}, dimensions={1}, use_global_device_ids=true | all-gather | bytes 557056 | tf_op jit(solution)/shard_map/all_gather | solution.py:49
  115.4 0.1 add_convert_fusion.1
  115.4 0.1 fusion.31
  115.5 0.2 multiply_cosine_fusion.1
  115.7 3.1 broadcast_in_dim.96
  118.8 11.8 %scatter_fusion = bf16[64,2,128,128]{3,2,1,0:T(8,128)(2,1)} fusion(bf16[64,2,128,128]{3,2,1,0:T(8,128)(2,1)} %broadcast_in_dim.96, s32[64]{0:T(128)S(1)} %fusion.49, bf16[64,2,128,128]{3,2,1,0:T(8,128)(2,1)} %bitcast.45), kind=kCustom, calls=%fused_computation.3 | custom fusion | bytes 12583168 | tf_op jit(solution)/shard_map/scatter | solution.py:70
  130.6 61.3 %all-gather.2.cloned.1.call-done = bf16[8192,1280]{1,0:T(8,128)(2,1)} async-done(((bf16[512,1280]{1,0:T(8,128)(2,1)}), bf16[8192,1280]{1,0:T(8,128)(2,1)}) %all-gather.2.cloned.1.call-update) | async-done | bytes 20971536 | tf_op jit(solution)/shard_map/all_gather | solution.py:52
  191.9 8.8 %fusion.56 = f32[32,1280]{1,0:T(8,128)S(1)} fusion(bf16[32,8192]{1,0:T(8,128)(2,1)S(1)} %all_gather.6, bf16[8192,1280]{1,0:T(8,128)(2,1)} %all-gather.2.cloned.1.call-done), kind=kOutput, calls=%fused_computation.106 | convolution fusion | flops 671088640 | bytes 21659648 | tf_op jit(solution)/shard_map/dot_general | solution.py:50
  200.7 0.1 subtract_convert_fusion
  200.9 0.1 maximum_bitcast_fusion
  201.0 0.7 gather_fusion
  201.6 2.9 fusion.54
  204.6 0.1 copy.64
  204.6 0.7 copy.66
  205.4 0.1 select_reduce_fusion
  205.5 0.1 copy.65
  205.5 38.1 %pmax.7 = f32[8,32]{1,0:T(8,128)S(1)} all-reduce(f32[8,32]{1,0:T(8,128)S(1)} %bitcast.130), channel_id=1, replica_groups=mesh['seq'=16,'head'=8] {'seq'}, use_global_device_ids=true, to_apply=%region_2.3 | all-reduce | flops 256 | bytes 2048 | tf_op jit(solution)/shard_map/pmax | solution.py:114
  243.7 1.2 gather_fusion.1
  244.9 0.7 copy.70
  245.6 0.7 copy.68
  246.3 0.8 fusion.15
  247.0 2.3 fusion
  249.3 0.4 reshape.416
  249.7 0.8 subtract_exponential_fusion
  250.5 0.3 mul.180
  250.9 1.8 fusion.7
  252.7 0.7 copy.69
  253.3 0.0 all-reduce.3.cloned.1.call-update
  253.3 0.9 fusion.45
  254.2 0.8 copy.73
  255.0 0.1 copy.76
  255.1 0.1 copy.77
  255.2 0.8 fusion.11
  256.0 0.1 copy.78
  256.1 0.1 copy.79
  256.2 36.0 %psum.15 = bf16[8,8,4]{1,2,0:T(4,128)(2,1)S(1)} all-reduce(bf16[8,8,4]{1,2,0:T(4,128)(2,1)S(1)} %copy.79), channel_id=1, replica_groups=mesh['seq'=16,'head'=8] {'seq'}, use_global_device_ids=true, to_apply=%region_6.7 | all-reduce | flops 256 | bytes 1024 | tf_op jit(solution)/shard_map/psum | solution.py:117
  292.2 1.4 fusion.55
  293.6 0.1 fusion.24
  293.8 36.9 %all-reduce.3.cloned.1.call-done = bf16[8,8,4,128]{3,1,2,0:T(8,128)(2,1)} async-done(((bf16[8,8,4,128]{3,1,2,0:T(8,128)(2,1)}), bf16[8,8,4,128]{3,1,2,0:T(8,128)(2,1)}) %all-reduce.3.cloned.1.call-update) | async-done | bytes 65552 | tf_op jit(solution)/shard_map/psum | solution.py:118
  330.7 1.1 fusion.8
  331.8 0.3 convolution_convert_fusion
  332.1 24.0 %all-reduce = bf16[32,512]{1,0:T(8,128)(2,1)S(1)} all-reduce(bf16[32,512]{1,0:T(8,128)(2,1)S(1)} %convolution_convert_fusion), channel_id=2, replica_groups=mesh['seq'=16,'head'=8] {'head'}, use_global_device_ids=true, to_apply=%region_8.9.clone | all-reduce | flops 16384 | bytes 65536
  356.1 0.6 constant_dynamic-slice_fusion
  (35 shorter events, 0.2 us)
Async XLA Ops:
  7.2 324.7 %copy-start = (bf16[1024,512]{1,0:T(8,128)(2,1)S(1)}, bf16[1024,512]{1,0:T(8,128)(2,1)}, u32[]{:S(2)}) copy-start(bf16[1024,512]{1,0:T(8,128)(2,1)} %param.11) | copy-start | bytes 3145732
  7.2 184.7 %all-gather.2.cloned.1.call-start = ((), (), s32[]{:S(2)}) async-start(), calls=%async_computation.1 | async-start | bytes 22282240 | tf_op jit(solution)/shard_map/all_gather | solution.py:52
  14.1 101.6 %all-to-all-start = ((bf16[16,4,2,128,128]{4,3,2,1,0:T(8,128)(2,1)}), bf16[16,4,2,128,128]{4,3,2,1,0:T(8,128)(2,1)}, u32[]{:S(2)}, u32[]{:S(2)}) async-start(bf16[16,4,2,128,128]{4,3,2,1,0:T(8,128)(2,1)} %bitcast.134), calls=%async_computation | async-start | bytes 8388608 | tf_op jit(solution)/shard_map/all_to_all | solution.py:68
  22.3 5.3 %copy-start.9 = (s32[1,16,4]{1,2,0:T(4,128)S(1)}, s32[1,16,4]{1,2,0:T(4,128)}, u32[]{:S(2)}) copy-start(s32[1,16,4]{1,2,0:T(4,128)} %param.17) | copy-start | bytes 772
  22.3 5.5 %copy-start.12 = (u32[128]{0:T(128)S(1)}, u32[128]{0:T(128)}, u32[]{:S(2)}) copy-start(u32[128]{0:T(128)} %constant.43) | copy-start | bytes 1540
  22.3 7.4 %copy-start.3 = (s32[8]{0:T(128)S(1)}, s32[8]{0:T(128)}, u32[]{:S(2)}) copy-start(s32[8]{0:T(128)} %param.13) | copy-start | bytes 100
  22.3 8.0 %copy-start.7 = (s32[64]{0:T(128)S(1)}, s32[64]{0:T(128)}, u32[]{:S(2)}) copy-start(s32[64]{0:T(128)} %param.14) | copy-start | bytes 772
  22.3 8.0 %copy-start.11 = (s32[64]{0:T(128)S(1)}, s32[64]{0:T(128)}, u32[]{:S(2)}) copy-start(s32[64]{0:T(128)} %param.15) | copy-start | bytes 772
  22.3 12.8 %copy-start.6 = (bf16[32,512]{1,0:T(8,128)(2,1)S(1)}, bf16[32,512]{1,0:T(8,128)(2,1)}, u32[]{:S(2)}) copy-start(bf16[32,512]{1,0:T(8,128)(2,1)} %param.9) | copy-start | bytes 98308
  22.4 308.4 %all-reduce.3.cloned.1.call-start = ((), (), s32[]{:S(2)}) async-start(), calls=%async_computation.2 | async-start | bytes 131072 | tf_op jit(solution)/shard_map/psum | solution.py:118
  29.1 101.5 %copy-start.8 = (f32[64]{0:T(128)}, f32[64]{0:T(128)S(1)}, u32[]{:S(2)}) copy-start(f32[64]{0:T(128)S(1)} %negate_power_fusion) | copy-start | bytes 772
  115.4 15.2 %copy-start.5 = (f32[8,4]{1,0:T(8,128)}, f32[8,4]{1,0:T(8,128)S(1)}, u32[]{:S(2)}) copy-start(f32[8,4]{1,0:T(8,128)S(1)} %add_convert_fusion.1) | copy-start | bytes 388
  200.8 0.8 copy-start.1
  200.9 0.8 copy-start.2
  244.9 2.1 copy-start.4
  249.7 43.9 %copy-start.10 = (pred[4,4]{1,0:T(4,128)(4,1)S(1)}, pred[4,4]{1,0:T(4,128)(4,1)}, u32[]{:S(2)}) copy-start(pred[4,4]{1,0:T(4,128)(4,1)} %iota_compare_fusion.3) | copy-start | bytes 52
Sparse Core Ops, SparseCore 0:
  10.1 181.6 all-gather.1
  253.4 77.2 all-reduce.2
where the time goes:
time: 365 us; the launch traced here: 364 us
  blocking collectives  178 us (49%)
  waiting for transfers between devices  98.9 us (27%)
  local copies, waits for them, and re-layouts  34.3 us (9%)
  matrix products  19.4 us (5%)
  between operations  15.1 us (4%)
  other arithmetic  9.38 us (3%)
  starting transfers between devices  8.26 us (2%)
    all_gather x1, blocking collectives, body(): full_rows = lax.all_gather(normed, 'seq', axis=1, tiled=True)  80.1 us
    all_gather x1, waiting for transfers between devices, body(): lax.all_gather(qkv_weight, 'seq', axis=0, tiled=True)  61.3 us
    pmax x1, blocking collectives, body(): total_max = lax.pmax(request_max, 'seq')  38.1 us
    psum x1, waiting for transfers between devices, body(): lax.psum((request_acc * adjust[:, :, None]).astype(jnp.bfloat16), 'seq')  36.9 us
    psum x1, blocking collectives, body(): lax.psum((request_sum * adjust).astype(jnp.bfloat16), 'seq')  36 us
    unnamed x1, blocking collectives  24 us
    scatter x1, local copies, waits for them, and re-layouts, body(): jnp.zeros_like(kv_cache).at[recv_list.reshape(-1)]  11.8 us
    dot_general x1, matrix products, body(): jnp.dot(full_rows, lax.all_gather(qkv_weight, 'seq', axis=0, tiled=True),...  8.79 us
  transfers between devices with their start and end apart: 3, of which 2 were waited for; matrix products, arithmetic and copies ran while one was open for 10% of the time, Pallas kernels for 0%

commit v1 on v0

--- a/solution.py
+++ b/solution.py
@@ -115,9 +115,9 @@
     adjust = jnp.exp(request_max - total_max)
     total_sum, total_acc = (
         lax.psum((request_sum * adjust).astype(jnp.bfloat16), "seq").astype(jnp.float32),
-        lax.psum((request_acc * adjust[:, :, None]).astype(jnp.bfloat16), "seq").astype(
-            jnp.float32
-        ),
+        jnp.sum(
+            lax.all_gather((request_acc * adjust[:, :, None]).astype(jnp.bfloat16), "seq"), axis=0
+        ).astype(jnp.float32),
     )
     new_scores = (
         jnp.einsum("rptgd,rqtd->rtgpq", queries, keys_new, preferred_element_type=jnp.float32)

time: 365 us -> 341 us (0.934)
  waiting for transfers between devices: 98.9 us -> 76.6 us
    psum x1 -> x0, waiting for transfers between devices: 36.9 us -> none  [body(): lax.psum((request_acc * adjust[:, :, None]).astype(jnp.bfloat16), 'seq')]
    all_gather x1, waiting for transfers between devices: 61.3 us -> 75.9 us  [body(): lax.all_gather(qkv_weight, 'seq', axis=0, tiled=True)]
    unnamed x30 -> x40, local copies, waits for them, and re-layouts: 6.56 us -> 8.26 us
  transfers between devices with their start and end apart: 3 -> 3, of which waited for: 2 -> 1; matrix products, arithmetic and copies ran while one was open for 10% -> 17% of each run, Pallas kernels for 0% -> 0%
where the time goes in v1:
time: 341 us; the launch traced here: 340 us
  blocking collectives  180 us (53%)
  waiting for transfers between devices  76.6 us (22%)
  local copies, waits for them, and re-layouts  33.3 us (10%)
  matrix products  17.5 us (5%)
  between operations  15.1 us (4%)
  other arithmetic  9.55 us (3%)
  starting transfers between devices  8.26 us (2%)
    all_gather x1, blocking collectives, body(): full_rows = lax.all_gather(normed, 'seq', axis=1, tiled=True)  82.1 us
    all_gather x1, waiting for transfers between devices, body(): lax.all_gather(qkv_weight, 'seq', axis=0, tiled=True)  75.9 us
    pmax x1, blocking collectives, body(): total_max = lax.pmax(request_max, 'seq')  38.1 us
    psum x1, blocking collectives, body(): lax.psum((request_sum * adjust).astype(jnp.bfloat16), 'seq')  36 us
    unnamed x1, blocking collectives  23.6 us
    scatter x1, local copies, waits for them, and re-layouts, body(): jnp.zeros_like(kv_cache).at[recv_list.reshape(-1)]  11.7 us
    dot_general x1, matrix products, body(): jnp.dot(full_rows, lax.all_gather(qkv_weight, 'seq', axis=0, tiled=True),...  8.8 us
    unnamed x40, local copies, waits for them, and re-layouts  8.26 us
  transfers between devices with their start and end apart: 3, of which 1 were waited for; matrix products, arithmetic and copies ran while one was open for 17% of the time, Pallas kernels for 0%

profile of v1, /device:TPU:0, one launch (start us, length us, event | category | flops | bytes accessed | tf_op | source)
XLA Modules:
  0.0 340.2 jit_solution(8442556454350314085)
XLA Ops:
  7.2 0.0 copy-start
  7.2 0.0 all-gather.4.cloned.1.call-start
  7.2 0.7 all-gather.4.cloned.1.call-update
  7.9 0.7 broadcast_minimum_fusion
  8.6 0.1 copy.80
  8.7 0.1 min.26
  8.8 5.2 %gather_fusion.2 = bf16[64,2,128,128]{3,2,1,0:T(8,128)(2,1)} fusion(bf16[64,2,128,128]{3,2,1,0:T(8,128)(2,1)} %param.12, s32[1024]{0:T(1024)S(1)} %pad_clamp_fusion), kind=kCustom, calls=%fused_computation.2 | custom fusion | bytes 8388864 | tf_op jit(solution)/shard_map/gather | solution.py:66
  14.0 8.2 %all-to-all-start = ((bf16[16,4,2,128,128]{4,3,2,1,0:T(8,128)(2,1)}), bf16[16,4,2,128,128]{4,3,2,1,0:T(8,128)(2,1)}, u32[]{:S(2)}, u32[]{:S(2)}) async-start(bf16[16,4,2,128,128]{4,3,2,1,0:T(8,128)(2,1)} %bitcast.135), calls=%async_computation | async-start | bytes 8388608 | tf_op jit(solution)/shard_map/all_to_all | solution.py:68
  22.2 0.0 copy-start.5
  22.2 0.0 copy-start.13
  22.3 0.0 copy-start.17
  22.3 0.0 copy-start.12
  22.3 0.0 all-gather.6.cloned.1.call-start
  22.3 5.3 %copy.113 = bf16[64,2,128,128]{3,2,0,1:T(8,128)(2,1)} copy(bf16[64,2,128,128]{3,2,1,0:T(8,128)(2,1)} %param.12) | data formatting | bytes 8388608 | tf_op args[3]
  27.6 0.7 fusion.53
  28.3 4.9 %compare_select_fusion.3 = (s32[64]{0:T(128)S(1)}, s32[64]{0:T(128)S(1)}, s32[64]{0:T(128)S(1)}) fusion(s32[]{:T(128)} %bitcast.1, s32[]{:T(128)} %bitcast.2, s32[]{:T(128)} %bitcast.3, s32[]{:T(128)} %bitcast.4, s32[]{:T(128)} %bitcast.5, s32[]{:T(128)} %bitcast.6, s32[]{:T(128)} %bitcast.7, s32[]{:T(128)} %bitcast.8, s32[64]{0:T(128)S(1)} %copy-done.13, ...), kind=kLoop, calls=%fused_computation.89 | loop fusion | flops 1216 | bytes 1312 | tf_op jit(solution)/shard_map/gather | solution.py:74
  33.2 82.1 %all_gather.12 = bf16[32,8192]{1,0:T(8,128)(2,1)S(1)} all-gather(bf16[32,512]{1,0:T(8,128)(2,1)S(1)} %copy-done.12), channel_id=1, replica_groups=mesh['seq'=16,'head'=8] {'seq'}, dimensions={1}, use_global_device_ids=true | all-gather | bytes 557056 | tf_op jit(solution)/shard_map/all_gather | solution.py:49
  115.3 0.1 add_convert_fusion.1
  115.4 0.1 fusion.31
  115.5 0.2 multiply_cosine_fusion.1
  115.7 0.3 copy-done.10
  116.0 75.9 %all-gather.4.cloned.1.call-done = bf16[8192,1280]{1,0:T(8,128)(2,1)} async-done(((bf16[512,1280]{1,0:T(8,128)(2,1)}), bf16[8192,1280]{1,0:T(8,128)(2,1)}) %all-gather.4.cloned.1.call-update) | async-done | bytes 20971536 | tf_op jit(solution)/shard_map/all_gather | solution.py:52
  191.8 8.8 %fusion.56 = f32[32,1280]{1,0:T(8,128)S(1)} fusion(bf16[32,8192]{1,0:T(8,128)(2,1)S(1)} %all_gather.12, bf16[8192,1280]{1,0:T(8,128)(2,1)} %all-gather.4.cloned.1.call-done), kind=kOutput, calls=%fused_computation.108 | convolution fusion | flops 671088640 | bytes 21659648 | tf_op jit(solution)/shard_map/dot_general | solution.py:50
  200.7 0.1 subtract_convert_fusion
  200.8 0.1 maximum_bitcast_fusion
  200.9 0.7 gather_fusion
  201.6 2.9 fusion.54
  204.5 0.1 copy.63
  204.6 0.7 copy.65
  205.3 0.1 select_reduce_fusion
  205.4 0.1 copy.64
  205.5 1.2 gather_fusion.1
  206.7 38.1 %pmax.7 = f32[8,32]{1,0:T(8,128)S(1)} all-reduce(f32[8,32]{1,0:T(8,128)S(1)} %bitcast.134), channel_id=1, replica_groups=mesh['seq'=16,'head'=8] {'seq'}, use_global_device_ids=true, to_apply=%region_2.3 | all-reduce | flops 256 | bytes 2048 | tf_op jit(solution)/shard_map/pmax | solution.py:114
  244.8 0.1 copy.67
  244.9 0.8 fusion.15
  245.7 0.0 copy-done.8
  245.7 2.3 fusion
  248.0 0.4 reshape.414
  248.4 0.8 subtract_exponential_fusion
  249.2 0.3 mul.180
  249.5 2.3 fusion.7
  251.9 0.0 all-gather.6.cloned.1.call-update
  251.9 0.8 copy.79
  252.6 0.1 reshape.421
  252.7 1.2 dynamic-slice
  254.7 3.1 broadcast_in_dim.96
  257.8 11.7 %scatter_fusion = bf16[64,2,128,128]{3,2,1,0:T(8,128)(2,1)} fusion(bf16[64,2,128,128]{3,2,1,0:T(8,128)(2,1)} %broadcast_in_dim.96, s32[64]{0:T(128)S(1)} %fusion.49, bf16[64,2,128,128]{3,2,1,0:T(8,128)(2,1)} %bitcast.46), kind=kCustom, calls=%fused_computation.3 | custom fusion | bytes 12583168 | tf_op jit(solution)/shard_map/scatter | solution.py:70
  269.5 0.1 copy.68
  269.6 0.1 copy.71
  269.7 0.1 copy.75
  269.7 0.1 copy.76
  269.9 0.1 fusion.11
  270.0 0.1 copy.77
  270.1 0.1 copy.78
  270.2 0.2 fusion.45
  270.4 0.5 fusion.55
  271.0 36.0 %psum.7 = bf16[8,8,4]{1,2,0:T(4,128)(2,1)S(1)} all-reduce(bf16[8,8,4]{1,2,0:T(4,128)(2,1)S(1)} %copy.78), channel_id=1, replica_groups=mesh['seq'=16,'head'=8] {'seq'}, use_global_device_ids=true, to_apply=%region_6.7 | all-reduce | flops 256 | bytes 1024 | tf_op jit(solution)/shard_map/psum | solution.py:117
  307.0 0.1 fusion.24
  307.1 0.0 all-gather.6.cloned.1.call-done
  307.1 1.4 bitcast_reduce_fusion
  308.5 0.3 fusion.8
  308.8 0.3 convolution_convert_fusion
  309.1 23.6 %all-reduce = bf16[32,512]{1,0:T(8,128)(2,1)S(1)} all-reduce(bf16[32,512]{1,0:T(8,128)(2,1)S(1)} %convolution_convert_fusion), channel_id=3, replica_groups=mesh['seq'=16,'head'=8] {'head'}, use_global_device_ids=true, to_apply=%region_8.9.clone | all-reduce | flops 16384 | bytes 65536
  332.7 0.6 constant_dynamic-slice_fusion
  (46 shorter events, 0.2 us)
Async XLA Ops:
  7.2 301.7 %copy-start = (bf16[1024,512]{1,0:T(8,128)(2,1)S(1)}, bf16[1024,512]{1,0:T(8,128)(2,1)}, u32[]{:S(2)}) copy-start(bf16[1024,512]{1,0:T(8,128)(2,1)} %param.11) | copy-start | bytes 3145732
  7.2 184.7 %all-gather.4.cloned.1.call-start = ((), (), s32[]{:S(2)}) async-start(), calls=%async_computation.1 | async-start | bytes 22282240 | tf_op jit(solution)/shard_map/all_gather | solution.py:52
  14.0 240.6 %all-to-all-start = ((bf16[16,4,2,128,128]{4,3,2,1,0:T(8,128)(2,1)}), bf16[16,4,2,128,128]{4,3,2,1,0:T(8,128)(2,1)}, u32[]{:S(2)}, u32[]{:S(2)}) async-start(bf16[16,4,2,128,128]{4,3,2,1,0:T(8,128)(2,1)} %bitcast.135), calls=%async_computation | async-start | bytes 8388608 | tf_op jit(solution)/shard_map/all_to_all | solution.py:68
  22.2 5.4 %copy-start.5 = (s32[8]{0:T(128)S(1)}, s32[8]{0:T(128)}, u32[]{:S(2)}) copy-start(s32[8]{0:T(128)} %param.13) | copy-start | bytes 100
  22.2 6.1 %copy-start.13 = (s32[64]{0:T(128)S(1)}, s32[64]{0:T(128)}, u32[]{:S(2)}) copy-start(s32[64]{0:T(128)} %param.14) | copy-start | bytes 772
  22.3 6.1 %copy-start.17 = (s32[64]{0:T(128)S(1)}, s32[64]{0:T(128)}, u32[]{:S(2)}) copy-start(s32[64]{0:T(128)} %param.15) | copy-start | bytes 772
  22.3 10.9 %copy-start.12 = (bf16[32,512]{1,0:T(8,128)(2,1)S(1)}, bf16[32,512]{1,0:T(8,128)(2,1)}, u32[]{:S(2)}) copy-start(bf16[32,512]{1,0:T(8,128)(2,1)} %param.9) | copy-start | bytes 98308
  22.3 284.8 %all-gather.6.cloned.1.call-start = ((), (), s32[]{:S(2)}) async-start(), calls=%async_computation.2 | async-start | bytes 1114112 | tf_op jit(solution)/shard_map/all_gather | solution.py:119
  27.6 88.0 %copy-start.15 = (f32[64]{0:T(128)}, f32[64]{0:T(128)S(1)}, u32[]{:S(2)}) copy-start(f32[64]{0:T(128)S(1)} %negate_power_fusion) | copy-start | bytes 772
  115.4 0.6 copy-start.10
  200.8 0.8 copy-start.1
  200.8 0.8 copy-start.3
  244.8 0.9 copy-start.8
  244.8 0.8 copy-start.6
  257.7 11.7 %copy-start.9 = (f32[8,32]{1,0:T(8,128)S(1)}, f32[8,32]{1,0:T(8,128)}, u32[]{:S(2)}) copy-start(f32[8,32]{1,0:T(8,128)} %copy-done.8) | copy-start | bytes 3076
  257.7 12.1 %copy-start.7 = (f32[8,32]{1,0:T(8,128)S(1)}, f32[8,32]{1,0:T(8,128)}, u32[]{:S(2)}) copy-start(f32[8,32]{1,0:T(8,128)} %copy-done.6) | copy-start | bytes 3076
  257.7 12.1 %copy-start.14 = (s32[64]{0:T(128)S(1)}, s32[64]{0:T(128)}, u32[]{:S(2)}) copy-start(s32[64]{0:T(128)} %param.14) | copy-start | bytes 772
  257.7 12.5 %copy-start.11 = (f32[8,4]{1,0:T(8,128)S(1)}, f32[8,4]{1,0:T(8,128)}, u32[]{:S(2)}) copy-start(f32[8,4]{1,0:T(8,128)} %copy-done.10) | copy-start | bytes 388
  257.7 12.5 %copy-start.16 = (f32[64]{0:T(128)S(1)}, f32[64]{0:T(128)}, u32[]{:S(2)}) copy-start(f32[64]{0:T(128)} %copy-done.15) | copy-start | bytes 772
  257.8 12.7 %copy-start.2 = (bf16[8,4,1,8,64]{4,3,1,0,2:T(8,128)(2,1)S(1)}, bf16[8,4,1,8,64]{4,3,1,0,2:T(8,128)(2,1)}, u32[]{:S(2)}) copy-start(bf16[8,4,1,8,64]{4,3,1,0,2:T(8,128)(2,1)} %copy-done.1) | copy-start | bytes 98308
  257.8 12.7 %copy-start.4 = (bf16[8,4,1,8,64]{4,3,1,0,2:T(8,128)(2,1)S(1)}, bf16[8,4,1,8,64]{4,3,1,0,2:T(8,128)(2,1)}, u32[]{:S(2)}) copy-start(bf16[8,4,1,8,64]{4,3,1,0,2:T(8,128)(2,1)} %copy-done.3) | copy-start | bytes 98308
Sparse Core Ops, SparseCore 0:
  10.1 181.6 all-gather.3
  252.0 39.8 all-gather.5
